TPU v7x, 32 devices: a whole 2x2x4 slice. The times are simulated.
32 devices in a mesh: dp: 4 (over y, x), ctx: 8 (over z, core).
Axes of the slice: x: 2, y: 2, z: 4, core: 2. Of those that a mesh axis runs over, the one named last changes fastest.
Arguments:
- tokens: bfloat16 [4, 1024, 1536], P('dp', 'ctx'), may hold values from -6 to 6
- positions: int32 [4, 1024], P('dp', 'ctx'), may hold values from 0 to 3071, as said below
- block_order: int32 [16], replicated, may hold values from 0 to 15, as said below
- cotangent: bfloat16 [4, 1024, 1536], P('dp', 'ctx'), may hold values from -6 to 6
- gain_attn: bfloat16 [1536], P('dp'), may hold values from 0.099609375 to 1.8984375
- w_qkv: bfloat16 [1536, 2048], P('dp'), may hold values from -0.15625 to 0.15625
- b_qkv: bfloat16 [2048], P('dp'), may hold values from -3 to 3
- w_out: bfloat16 [1536, 1536], P('dp'), may hold values from -1.75 to 1.75
- gain_mlp: bfloat16 [1536], P('dp'), may hold values from 0.099609375 to 1.8984375
- w_gate: bfloat16 [1536, 8960], P('dp'), may hold values from -0.15625 to 0.15625
- w_up: bfloat16 [1536, 8960], P('dp'), may hold values from -0.15625 to 0.15625
- w_down: bfloat16 [8960, 1536], P('dp'), may hold values from -0.0625 to 0.0625
Outputs:
- block_out: bfloat16 [4, 1024, 1536], P('dp', 'ctx')
- grad_tokens: float32 [4, 1024, 1536], P('dp', 'ctx')
- grad_gain_attn: float32 [1536], P(('dp', 'ctx'))
- grad_w_qkv: float32 [1536, 2048], P(('dp', 'ctx'))
- grad_b_qkv: float32 [2048], P(('dp', 'ctx'))
- grad_w_out: float32 [1536, 1536], P(('dp', 'ctx'))
- grad_gain_mlp: float32 [1536], P(('dp', 'ctx'))
- grad_w_gate: float32 [1536, 8960], P(('dp', 'ctx'))
- grad_w_up: float32 [1536, 8960], P(('dp', 'ctx'))
- grad_w_down: float32 [8960, 1536], P(('dp', 'ctx'))
Inputs may be any that keep to these rules, and one draw needn't show every extreme that they name: A permutation in which entries 2c and 2c + 1 always add up to 15; the device of index c along ctx stores, as its first and its second 64 tokens of every sequence, that sequence's sub-blocks block_order[2c] and block_order[2c + 1]. positions[s, t] is an offset of sequence s, from 0 to 2048, plus the index idx(t) of the token stored at place t; the first sequence's offset is 0 and the last one's 2 * 1024.
All inputs are finite; a program needn't handle non-finite values.
Results may differ from a plain program's by a relative error of at most 0.02.
Values may be sent and summed in bfloat16 or wider, within the bound.
No kernel may reach another device: no remote copies, remote signals or barrier semaphores. Data moves between devices by JAX's collectives and lax.ppermute only.
A program may use at most 576 MiB of HBM per device.

v0:
```python
import math
import jax
import jax.numpy as jnp
from jax import lax
from jax.sharding import PartitionSpec as P

HEADS = 12
KV_HEADS = 2
HEAD_DIM = 128
rope_base = 1000000.0
norm_eps = 1e-06
masked_score = -1e30


def from_behind(value, axis, steps):
    count = lax.axis_size(axis)
    pairs = [(source, (source + steps) % count) for source in range(count)]
    return lax.ppermute(value, axis, pairs)


def normalize(rows_in, gain):
    inverse = lax.rsqrt(jnp.mean(rows_in * rows_in, axis=-1, keepdims=True) + norm_eps)
    normed = rows_in * inverse
    return (normed, inverse, (normed * gain.astype(jnp.float32)).astype(jnp.bfloat16))


def normalize_back(grad_out, normed, inverse, gain):
    scaled = grad_out * gain.astype(jnp.float32)
    grad_rows = inverse * (scaled - normed * jnp.mean(scaled * normed, axis=-1, keepdims=True))
    return (grad_rows, jnp.sum(grad_out * normed, axis=0))


def rope_tables(token_positions, head_dim):
    half_dim = head_dim // 2
    half_steps = jnp.arange(half_dim, dtype=jnp.float32)
    frequency = jnp.exp(-math.log(rope_base) * (2.0 * half_steps / head_dim))
    angles = token_positions.astype(jnp.float32)[:, None] * frequency[None, :]
    return (jnp.cos(angles), jnp.sin(angles))


def rotate(head_rows, cosines, sines):
    half_dim = head_rows.shape[-1] // 2
    front_half = head_rows[..., :half_dim]
    back_half = head_rows[..., half_dim:]
    cosine_part = cosines[:, None, :]
    sine_part = sines[:, None, :]
    return jnp.concatenate(
        [
            front_half * cosine_part - back_half * sine_part,
            back_half * cosine_part + front_half * sine_part,
        ],
        axis=-1,
    )


def unrotate(grad_rows, cosines, sines):
    half_dim = grad_rows.shape[-1] // 2
    front_half = grad_rows[..., :half_dim]
    back_half = grad_rows[..., half_dim:]
    cosine_part = cosines[:, None, :]
    sine_part = sines[:, None, :]
    return jnp.concatenate(
        [
            front_half * cosine_part + back_half * sine_part,
            back_half * cosine_part - front_half * sine_part,
        ],
        axis=-1,
    )


def logical_index(places, block_order, sub_len):
    slot_index = places // sub_len
    slot_match = slot_index[:, None] == jnp.arange(block_order.shape[0], dtype=jnp.int32)[None, :]
    blocks = jnp.sum(jnp.where(slot_match, block_order[None, :], 0), axis=1)
    return blocks * sub_len + places % sub_len


def block_scores(queries, key_rows, allowed, score_scale):
    scores = (
        jnp.einsum("skgtd,sukd->skgtu", queries, key_rows, preferred_element_type=jnp.float32)
        * score_scale
    )
    return jnp.where(allowed, scores, masked_score)


def attend(softmax_state, queries, kv_pair, allowed, score_scale):
    running, total_mass, summed = softmax_state
    scores = block_scores(queries, kv_pair[0], allowed, score_scale)
    newest = jnp.maximum(running, jnp.max(scores, axis=-1))
    factor = jnp.exp(running - newest)
    unscaled = jnp.exp(scores - newest[..., None])
    total_mass = total_mass * factor + jnp.sum(unscaled, axis=-1)
    summed = summed * factor[..., None] + jnp.einsum(
        "skgtu,sukd->skgtd",
        unscaled.astype(jnp.bfloat16),
        kv_pair[1],
        preferred_element_type=jnp.float32,
    )
    return (newest, total_mass, summed)


def attend_back(queries, kv_pair, allowed, log_total, grad_heads, delta, score_scale):
    scores = block_scores(queries, kv_pair[0], allowed, score_scale)
    probs_full = jnp.where(allowed, jnp.exp(scores - log_total[..., None]), 0.0)
    grad_probs = jnp.einsum(
        "skgtd,sukd->skgtu", grad_heads, kv_pair[1], preferred_element_type=jnp.float32
    )
    grad_scores = (probs_full * (grad_probs - delta[..., None])).astype(jnp.bfloat16)
    grad_query = (
        jnp.einsum("skgtu,sukd->skgtd", grad_scores, kv_pair[0], preferred_element_type=jnp.float32)
        * score_scale
    )
    grad_key = (
        jnp.einsum("skgtu,skgtd->sukd", grad_scores, queries, preferred_element_type=jnp.float32)
        * score_scale
    )
    grad_value = jnp.einsum(
        "skgtu,skgtd->sukd",
        probs_full.astype(jnp.bfloat16),
        grad_heads,
        preferred_element_type=jnp.float32,
    )
    return (grad_query, jnp.stack([grad_key, grad_value]))


def body(
    tokens,
    positions,
    block_order,
    cotangent,
    gain_attn,
    w_qkv,
    b_qkv,
    w_out,
    gain_mlp,
    w_gate,
    w_up,
    w_down,
):
    seq_count, tok_count, width = tokens.shape
    row_count = seq_count * tok_count
    ctx_count = lax.axis_size("ctx")
    ctx_place = lax.axis_index("ctx")
    groups = HEADS // KV_HEADS
    query_width = HEADS * HEAD_DIM
    kv_width = KV_HEADS * HEAD_DIM
    proj_width = query_width + 2 * kv_width
    score_scale = 1.0 / math.sqrt(HEAD_DIM)
    sub_len = tok_count // 2
    local_places = jnp.arange(tok_count, dtype=jnp.int32)
    own_index = logical_index(ctx_place * tok_count + local_places, block_order, sub_len)

    def visible(places):
        return logical_index(places, block_order, sub_len)[None, :] <= own_index[:, None]

    gain_one, qkv_full, bias_full, out_full = (
        lax.all_gather(gain_attn, "dp", axis=0, tiled=True),
        lax.all_gather(w_qkv, "dp", axis=0, tiled=True),
        lax.all_gather(b_qkv, "dp", axis=0, tiled=True),
        lax.all_gather(w_out, "dp", axis=0, tiled=True),
    )
    inputs = tokens.reshape(row_count, width).astype(jnp.float32)
    normed_one, inverse_one, hidden_one = normalize(inputs, gain_one)
    projected = jnp.dot(
        hidden_one, qkv_full, preferred_element_type=jnp.float32
    ) + bias_full.astype(jnp.float32)
    cosines, sines = rope_tables(positions.reshape(row_count), HEAD_DIM)
    query_rot = rotate(
        projected[:, :query_width].reshape(row_count, HEADS, HEAD_DIM), cosines, sines
    )
    key_rot = rotate(
        projected[:, query_width : query_width + kv_width].reshape(row_count, KV_HEADS, HEAD_DIM),
        cosines,
        sines,
    )
    value_part = projected[:, query_width + kv_width :]
    queries = (
        query_rot.astype(jnp.bfloat16)
        .reshape(seq_count, tok_count, KV_HEADS, groups, HEAD_DIM)
        .transpose(0, 2, 3, 1, 4)
    )
    key_rows = key_rot.astype(jnp.bfloat16).reshape(seq_count, tok_count, KV_HEADS, HEAD_DIM)
    value_rows = value_part.astype(jnp.bfloat16).reshape(seq_count, tok_count, KV_HEADS, HEAD_DIM)
    kv_pair = jnp.stack([key_rows, value_rows])
    start_state = (
        jnp.full((seq_count, KV_HEADS, groups, tok_count), masked_score, jnp.float32),
        jnp.zeros((seq_count, KV_HEADS, groups, tok_count), jnp.float32),
        jnp.zeros((seq_count, KV_HEADS, groups, tok_count, HEAD_DIM), jnp.float32),
    )

    def cycle_step(step_index, loop_carry):
        softmax_state, pair_now = loop_carry
        source = (ctx_place - step_index) % ctx_count
        allowed = visible(source * tok_count + local_places)
        softmax_state = attend(softmax_state, queries, pair_now, allowed, score_scale)
        pair_now = from_behind(pair_now, "ctx", 1)
        return (softmax_state, pair_now)

    softmax_state, pair_last = lax.fori_loop(0, ctx_count - 1, cycle_step, (start_state, kv_pair))
    source_last = (ctx_place - (ctx_count - 1)) % ctx_count
    softmax_state = attend(
        softmax_state,
        queries,
        pair_last,
        visible(source_last * tok_count + local_places),
        score_scale,
    )
    running, total_mass, summed = softmax_state
    attn_rows = summed / total_mass[..., None]
    log_total = running + jnp.log(total_mass)
    attn_flat = (
        attn_rows.astype(jnp.bfloat16).transpose(0, 3, 1, 2, 4).reshape(row_count, query_width)
    )
    middle = inputs + jnp.dot(attn_flat, out_full, preferred_element_type=jnp.float32)
    gain_two, gate_full, up_full, down_full = (
        lax.all_gather(gain_mlp, "dp", axis=0, tiled=True),
        lax.all_gather(w_gate, "dp", axis=0, tiled=True),
        lax.all_gather(w_up, "dp", axis=0, tiled=True),
        lax.all_gather(w_down, "dp", axis=0, tiled=True),
    )
    normed_two, inverse_two, hidden_two = normalize(middle, gain_two)
    gate_values = jnp.dot(hidden_two, gate_full, preferred_element_type=jnp.float32)
    up_values = jnp.dot(hidden_two, up_full, preferred_element_type=jnp.float32)
    sigmoid_gate = jax.nn.sigmoid(gate_values)
    activated = (gate_values * sigmoid_gate * up_values).astype(jnp.bfloat16)
    result = middle + jnp.dot(activated, down_full, preferred_element_type=jnp.float32)
    block_out = result.astype(jnp.bfloat16).reshape(seq_count, tok_count, width)
    grad_top = cotangent.reshape(row_count, width)
    gain_two_b, gate_b, up_b, down_b = (
        lax.all_gather(gain_mlp, "dp", axis=0, tiled=True),
        lax.all_gather(w_gate, "dp", axis=0, tiled=True),
        lax.all_gather(w_up, "dp", axis=0, tiled=True),
        lax.all_gather(w_down, "dp", axis=0, tiled=True),
    )
    left_part = activated
    down_share = lax.psum_scatter(
        jnp.einsum("rf,rd->fd", left_part, grad_top, preferred_element_type=jnp.float32),
        ("dp", "ctx"),
        scatter_dimension=0,
        tiled=True,
    )
    grad_act = jnp.einsum("rd,fd->rf", grad_top, down_b, preferred_element_type=jnp.float32)
    grad_gate = (
        grad_act * up_values * sigmoid_gate * (1.0 + gate_values * (1.0 - sigmoid_gate))
    ).astype(jnp.bfloat16)
    grad_up = (grad_act * gate_values * sigmoid_gate).astype(jnp.bfloat16)
    grad_gate_up = jnp.concatenate([grad_gate, grad_up], axis=1)
    left_part = hidden_two
    gate_up_share = lax.psum_scatter(
        jnp.einsum("rd,rf->df", left_part, grad_gate_up, preferred_element_type=jnp.float32),
        ("dp", "ctx"),
        scatter_dimension=0,
        tiled=True,
    )
    ff_width = gate_full.shape[1]
    gate_share = gate_up_share[:, :ff_width]
    up_share = gate_up_share[:, ff_width:]
    grad_hidden_two = jnp.einsum(
        "rf,df->rd", grad_gate, gate_b, preferred_element_type=jnp.float32
    ) + jnp.einsum("rf,df->rd", grad_up, up_b, preferred_element_type=jnp.float32)
    grad_middle_norm, grad_gain_two = normalize_back(
        grad_hidden_two, normed_two, inverse_two, gain_two_b
    )
    grad_middle = grad_top.astype(jnp.float32) + grad_middle_norm
    gain_one_b, qkv_b, bias_b, out_b = (
        lax.all_gather(gain_attn, "dp", axis=0, tiled=True),
        lax.all_gather(w_qkv, "dp", axis=0, tiled=True),
        lax.all_gather(b_qkv, "dp", axis=0, tiled=True),
        lax.all_gather(w_out, "dp", axis=0, tiled=True),
    )
    grad_branch = grad_middle.astype(jnp.bfloat16)
    grad_attn = jnp.einsum(
        "rd,qd->rq", grad_branch, out_b, preferred_element_type=jnp.float32
    ).astype(jnp.bfloat16)
    grad_heads = grad_attn.reshape(seq_count, tok_count, KV_HEADS, groups, HEAD_DIM).transpose(
        0, 2, 3, 1, 4
    )
    delta = jnp.sum(grad_heads.astype(jnp.float32) * attn_rows, axis=-1)
    zero_query = jnp.zeros((seq_count, KV_HEADS, groups, tok_count, HEAD_DIM), jnp.float32)
    zero_pair = jnp.zeros((2, seq_count, tok_count, KV_HEADS, HEAD_DIM), jnp.float32)

    def back_step(step_index, loop_carry):
        grad_query, pair_now, grad_pair = loop_carry
        source = (ctx_place - step_index) % ctx_count
        allowed = visible(source * tok_count + local_places)
        part_query, part_pair = attend_back(
            queries, pair_now, allowed, log_total, grad_heads, delta, score_scale
        )
        pair_now = from_behind(pair_now, "ctx", 1)
        grad_pair = from_behind((grad_pair + part_pair).astype(jnp.bfloat16), "ctx", 1).astype(
            jnp.float32
        )
        return (grad_query + part_query, pair_now, grad_pair)

    grad_query, pair_home, grad_pair = lax.fori_loop(
        0, ctx_count, back_step, (zero_query, kv_pair, zero_pair)
    )
    grad_query_rows = grad_query.transpose(0, 3, 1, 2, 4).reshape(row_count, HEADS, HEAD_DIM)
    grad_query_raw = unrotate(grad_query_rows, cosines, sines).reshape(row_count, query_width)
    grad_key_raw = unrotate(
        grad_pair[0].reshape(row_count, KV_HEADS, HEAD_DIM), cosines, sines
    ).reshape(row_count, kv_width)
    grad_proj = jnp.concatenate(
        [grad_query_raw, grad_key_raw, grad_pair[1].reshape(row_count, kv_width)], axis=1
    ).astype(jnp.bfloat16)
    grad_bias = jnp.sum(grad_proj.astype(jnp.float32), axis=0)
    grad_hidden_one = jnp.einsum("rc,dc->rd", grad_proj, qkv_b, preferred_element_type=jnp.float32)
    grad_input_norm, grad_gain_one = normalize_back(
        grad_hidden_one, normed_one, inverse_one, gain_one_b
    )
    grad_tokens = (grad_middle + grad_input_norm).reshape(seq_count, tok_count, width)
    attn_share = lax.psum_scatter(
        jnp.concatenate(
            [
                jnp.einsum("rd,rc->dc", hidden_one, grad_proj, preferred_element_type=jnp.float32),
                jnp.einsum("rq,rd->qd", attn_flat, grad_branch, preferred_element_type=jnp.float32),
            ],
            axis=1,
        ),
        ("dp", "ctx"),
        scatter_dimension=0,
        tiled=True,
    )
    qkv_share = attn_share[:, :proj_width]
    out_share = attn_share[:, proj_width:]
    gain_one_share, bias_share, gain_two_share = (
        lax.psum_scatter(grad_gain_one, ("dp", "ctx"), scatter_dimension=0, tiled=True),
        lax.psum_scatter(grad_bias, ("dp", "ctx"), scatter_dimension=0, tiled=True),
        lax.psum_scatter(grad_gain_two, ("dp", "ctx"), scatter_dimension=0, tiled=True),
    )
    return (
        block_out,
        grad_tokens,
        gain_one_share,
        qkv_share,
        bias_share,
        out_share,
        gain_two_share,
        gate_share,
        up_share,
        down_share,
    )


def solution(mesh):
    return jax.shard_map(
        body,
        mesh=mesh,
        in_specs=(
            P("dp", "ctx", None),
            P("dp", "ctx"),
            P(),
            P("dp", "ctx", None),
            P("dp"),
            P("dp", None),
            P("dp"),
            P("dp", None),
            P("dp"),
            P("dp", None),
            P("dp", None),
            P("dp", None),
        ),
        out_specs=(
            P("dp", "ctx", None),
            P("dp", "ctx", None),
            P(("dp", "ctx")),
            P(("dp", "ctx"), None),
            P(("dp", "ctx")),
            P(("dp", "ctx"), None),
            P(("dp", "ctx")),
            P(("dp", "ctx"), None),
            P(("dp", "ctx"), None),
            P(("dp", "ctx"), None),
        ),
        check_vma=False,
    )
```

profile of v0, /device:TPU:0, one launch (start us, length us, event | category | flops | bytes accessed | tf_op | source)
XLA Modules:
  0.0 2639.6 jit_solution(16025676978261663640)
XLA Ops:
  10.8 9.6 all-gather.2
  21.0 8.3 all-gather
  29.4 7.4 all-gather.1
  38.1 44.6 %all-gather.9.cloned.1.call-done = bf16[1536,2048]{1,0:T(8,128)(2,1)} async-done(((bf16[384,2048]{1,0:T(8,128)(2,1)}), bf16[1536,2048]{1,0:T(8,128)(2,1)}) %all-gather.9.cloned.1.call-update) | async-done | bytes 6291472 | tf_op jit(solution)/shard_map/all_gather | solution.py:158
  93.4 44.1 %while.44 = (s32[]{:T(128)}, f32[1,2,6,128]{3,2,1,0:T(8,128)S(1)}, f32[1,2,6,128]{3,2,1,0:T(8,128)S(1)}, f32[1,2,6,128,128]{4,3,2,1,0:T(8,128)S(1)}, bf16[2,1,12...) while((s32[]{:T(128)}, f32[1,2,6,128]{3,2,1,0:T(8,128)S(1)}, ...), condition=%wide.region_6.7_spmd.clone, body=%wide.region_2.6_spmd.clone.sunk | while | flops 102664848 | bytes 5382022 | solution.py:199
  146.9 243.6 %all-gather.15.cloned.1.call-done = bf16[1536,8960]{1,0:T(8,128)(2,1)} async-done(((bf16[384,8960]{1,0:T(8,128)(2,1)}), bf16[1536,8960]{1,0:T(8,128)(2,1)}) %all-gather.15.cloned.1.call-update) | async-done | bytes 27525136 | tf_op jit(solution)/shard_map/all_gather | solution.py:218
  390.4 15.8 fusion.96
  406.3 232.9 %all-gather.13.cloned.1.call-done = bf16[1536,8960]{1,0:T(8,128)(2,1)} async-done(((bf16[384,8960]{1,0:T(8,128)(2,1)}), bf16[1536,8960]{1,0:T(8,128)(2,1)}) %all-gather.13.cloned.1.call-update) | async-done | bytes 27525136 | tf_op jit(solution)/shard_map/all_gather | solution.py:217
  639.2 15.8 fusion.95
  655.0 232.9 %all-gather.17.cloned.1.call-done = bf16[8960,1536]{1,0:T(8,128)(2,1)} async-done(((bf16[2240,1536]{1,0:T(8,128)(2,1)}), bf16[8960,1536]{1,0:T(8,128)(2,1)}) %all-gather.17.cloned.1.call-update) | async-done | bytes 27525136 | tf_op jit(solution)/shard_map/all_gather | solution.py:219
  887.9 19.0 multiply_convert_fusion
  906.9 14.5 fusion.97
  921.4 16.0 multiply_reduce_fusion
  946.4 90.3 %while.45 = (s32[]{:T(128)}, f32[1,2,6,128,128]{4,3,2,1,0:T(8,128)S(1)}, bf16[2,1,128,2,128]{4,2,3,1,0:T(8,128)(2,1)}, f32[2,1,128,2,128]{4,2,3,1,0:T(8,128)S(1)...) while((s32[]{:T(128)}, ...), condition=%wide.region_15.16_spmd.clone, body=%wide.region_13.15_spmd.clone.sunk | while | flops 254207632 | bytes 9553853 | solution.py:295
  961.9 6.2 collective-permute-done.2
  973.1 6.2 collective-permute-done.2
  1048.4 7.9 pad_maximum_fusion
  1057.2 50.7 %fusion.42 = f32[1536,17920]{1,0:T(8,128)} fusion(bf16[128,1536]{1,0:T(8,128)(2,1)S(1)} %copy-done.3, bf16[128,8960]{1,0:T(8,128)(2,1)} %get-tuple-element.822, bf16[128,8960]{1,0:T(8,128)(2,1)} %get-tuple-element.823), kind=kOutput, calls=%fused_computation.72 | convolution fusion | flops 7055605760 | bytes 115081216 | tf_op jit(solution)/shard_map/rd,rf->df/dot_general | solution.py:250
  1109.0 23.7 fusion.67
  1139.0 40.6 %all-reduce.4 = (f32[1536]{0:T(1024)S(1)}, f32[2048]{0:T(1024)S(1)}, f32[1536]{0:T(1024)S(1)}) all-reduce(f32[1536]{0:T(1024)S(1)} %get-tuple-element.771, f32[2048]{0:T(1024)S(1)} %convert_reduce_fusion, f32[1536]{0:T(1024)S(1)} %copy-done.18), channel_id=2, replica_groups=mesh['dp'=4,'ctx'=8] {'dp','ctx'}, use_global_device_ids=true, to_apply=%region_18.19.clone | all-reduce | flops 5120 | bytes 40960
  1183.6 15.0 fusion.47
  1198.6 81.3 %reduce-scatter.6.cloned.1.call-done = f32[48,3584]{1,0:T(8,128)} async-done(((f32[1536,3584]{1,0:T(8,128)}), f32[48,3584]{1,0:T(8,128)}) %reduce-scatter.6.cloned.1.call-update) | async-done | bytes 688144 | tf_op jit(solution)/shard_map/reduce_scatter | solution.py:312
  1283.3 883.2 %reduce-scatter.8.cloned.1.call-done = f32[48,17920]{1,0:T(8,128)} async-done(((f32[1536,17920]{1,0:T(8,128)}), f32[48,17920]{1,0:T(8,128)}) %reduce-scatter.8.cloned.1.call-update) | async-done | bytes 3440656 | tf_op jit(solution)/shard_map/reduce_scatter | solution.py:249
  2170.5 462.1 %reduce-scatter.10.cloned.1.call-done = f32[280,1536]{1,0:T(8,128)} async-done(((f32[8960,1536]{1,0:T(8,128)}), f32[280,1536]{1,0:T(8,128)}) %reduce-scatter.10.cloned.1.call-update) | async-done | bytes 1720336
  (369 shorter events, 185.7 us)
Async XLA Ops:
  7.2 75.5 %all-gather.9.cloned.1.call-start = ((), (), s32[]{:S(2)}) async-start(), calls=%async_computation.3 | async-start | bytes 7864320 | tf_op jit(solution)/shard_map/all_gather | solution.py:158
  7.9 135.4 %all-gather.11.cloned.1.call-start = ((), (), s32[]{:S(2)}) async-start(), calls=%async_computation.4 | async-start | bytes 5898240 | tf_op jit(solution)/shard_map/all_gather | solution.py:160
  8.7 381.8 %all-gather.15.cloned.1.call-start = ((), (), s32[]{:S(2)}) async-start(), calls=%async_computation.6 | async-start | bytes 34406400 | tf_op jit(solution)/shard_map/all_gather | solution.py:218
  9.4 629.8 %all-gather.13.cloned.1.call-start = ((), (), s32[]{:S(2)}) async-start(), calls=%async_computation.5 | async-start | bytes 34406400 | tf_op jit(solution)/shard_map/all_gather | solution.py:217
  10.0 877.9 %all-gather.17.cloned.1.call-start = ((), (), s32[]{:S(2)}) async-start(), calls=%async_computation.7 | async-start | bytes 34406400 | tf_op jit(solution)/shard_map/all_gather | solution.py:219
  10.6 1269.3 %reduce-scatter.6.cloned.1.call-start = ((), (), s32[]{:S(2)}) async-start(), calls=%async_computation.8 | async-start | bytes 22708224 | tf_op jit(solution)/shard_map/reduce_scatter | solution.py:312
  947.4 10.3 collective-permute-start.1
  950.2 6.5 collective-permute-start.2
  958.6 10.3 collective-permute-start.1
  961.5 6.5 collective-permute-start.2
  969.9 10.3 collective-permute-start.1
  972.8 6.5 collective-permute-start.2
  981.2 10.3 collective-permute-start.1
  984.1 6.5 collective-permute-start.2
  992.4 10.3 collective-permute-start.1
  995.3 6.5 collective-permute-start.2
  1003.7 10.3 collective-permute-start.1
  1006.6 6.5 collective-permute-start.2
  1015.0 10.3 collective-permute-start.1
  1017.9 6.5 collective-permute-start.2
  1026.2 10.3 collective-permute-start.1
  1029.1 6.5 collective-permute-start.2
  1056.3 1110.3 %reduce-scatter.8.cloned.1.call-start = ((), (), s32[]{:S(2)}) async-start(), calls=%async_computation.9 | async-start | bytes 113541120 | tf_op jit(solution)/shard_map/reduce_scatter | solution.py:249
  1108.0 1524.6 %reduce-scatter.10.cloned.1.call-start = ((), (), s32[]{:S(2)}) async-start(), calls=%async_computation.10 | async-start | bytes 56770560
  (37 other events, 1740.8 us)
Sparse Core Ops, SparseCore 0:
  9.8 72.8 all-gather.8
  84.6 56.9 all-gather.10
  143.4 247.0 all-gather.14
  392.2 246.9 all-gather.12
  640.9 246.9 all-gather.16
  1056.4 223.4 reduce-scatter.5
  1286.3 880.1 reduce-scatter.7
  2173.5 459.0 reduce-scatter.9
where the time goes:
time: 2640 us
  waiting for transfers between devices  2260 us (86%)
  matrix products  223 us (8%)
  blocking collectives  65.9 us (2%)
  other arithmetic  40.8 us (2%)
  local copies, waits for them, and re-layouts  28.8 us (1%)
    reduce_scatter x1, waiting for transfers between devices, body(): lax.psum_scatter(jnp.einsum('rd,rf->df', left_part, grad_gate_up, preferr...  883 us
    unnamed x9, waiting for transfers between devices  465 us
    all_gather x1, waiting for transfers between devices, body(): lax.all_gather(w_up, 'dp', axis=0, tiled=True)  244 us
    all_gather x1, waiting for transfers between devices, body(): lax.all_gather(w_gate, 'dp', axis=0, tiled=True)  233 us
    all_gather x1, waiting for transfers between devices, body(): lax.all_gather(w_down, 'dp', axis=0, tiled=True)  233 us
    reduce_scatter x1, waiting for transfers between devices, body(): lax.psum_scatter(jnp.concatenate([jnp.einsum('rd,rc->dc', hidden_one, gra...  81.3 us
    ppermute x23, waiting for transfers between devices, from_behind(): return lax.ppermute(value, axis, pairs)  77.9 us
  transfers between devices with their start and end apart: 31, of which 22 were waited for; matrix products, arithmetic and copies ran while one was open for 8% of the time, Pallas kernels for 0%

commit v1 on v0

--- a/solution.py
+++ b/solution.py
@@ -10,6 +10,18 @@
 rope_base = 1000000.0
 norm_eps = 1e-06
 masked_score = -1e30
+
+
+def doubled_up(x, axis, dim):
+    ways, here, hop = (lax.axis_size(axis), lax.axis_index(axis), x.shape[dim])
+    line, have = (x, 1)
+    while have < ways:
+        line = jnp.concatenate(
+            [line, lax.ppermute(line, axis, [(d, (d - have) % ways) for d in range(ways)])],
+            axis=dim,
+        )
+        have = 2 * have
+    return jnp.roll(line, here * hop, axis=dim)
 
 
 def from_behind(value, axis, steps):
@@ -216,7 +228,7 @@
         lax.all_gather(gain_mlp, "dp", axis=0, tiled=True),
         lax.all_gather(w_gate, "dp", axis=0, tiled=True),
         lax.all_gather(w_up, "dp", axis=0, tiled=True),
-        lax.all_gather(w_down, "dp", axis=0, tiled=True),
+        doubled_up(w_down, "dp", 0),
     )
     normed_two, inverse_two, hidden_two = normalize(middle, gain_two)
     gate_values = jnp.dot(hidden_two, gate_full, preferred_element_type=jnp.float32)

time: 2640 us -> 2760 us (1.045)
  waiting for transfers between devices: 2260 us -> 2320 us
  local copies, waits for them, and re-layouts: 28.8 us -> 63.1 us
    ppermute x0 -> x2, waiting for transfers between devices: none -> 520 us  [doubled_up(): lax.ppermute(line, axis, [(d, (d - have) % ways) for d in range(ways)])]
    reduce_scatter x1, waiting for transfers between devices: 883 us -> 501 us  [body(): lax.psum_scatter(jnp.einsum('rd,rf->df', left_part, grad_gate_up, preferr...]
    reduce_scatter x1, waiting for transfers between devices: 81.3 us -> 0.01 us  [body(): lax.psum_scatter(jnp.concatenate([jnp.einsum('rd,rc->dc', hidden_one, gra...]
    unnamed x69 -> x118, local copies, waits for them, and re-layouts: 7.33 us -> 37.9 us
  transfers between devices with their start and end apart: 31 -> 33, of which waited for: 22 -> 24; matrix products, arithmetic and copies ran while one was open for 8% -> 9% of each run, Pallas kernels for 0% -> 0%
where the time goes in v1:
time: 2760 us; the launch traced here: 2750 us
  waiting for transfers between devices  2320 us (84%)
  matrix products  219 us (8%)
  blocking collectives  79.7 us (3%)
  local copies, waits for them, and re-layouts  63.1 us (2%)
  other arithmetic  39.8 us (1%)
    ppermute x2, waiting for transfers between devices, doubled_up(): lax.ppermute(line, axis, [(d, (d - have) % ways) for d in range(ways)])  520 us
    reduce_scatter x1, waiting for transfers between devices, body(): lax.psum_scatter(jnp.einsum('rd,rf->df', left_part, grad_gate_up, preferr...  501 us
    unnamed x9, waiting for transfers between devices  465 us
    all_gather x1, waiting for transfers between devices, body(): lax.all_gather(w_gate, 'dp', axis=0, tiled=True)  245 us
    all_gather x1, waiting for transfers between devices, body(): lax.all_gather(w_up, 'dp', axis=0, tiled=True)  233 us
    all_gather x1, waiting for transfers between devices, body(): lax.all_gather(w_down, 'dp', axis=0, tiled=True)  233 us
    ppermute x23, waiting for transfers between devices, from_behind(): return lax.ppermute(value, axis, pairs)  79.8 us
  transfers between devices with their start and end apart: 33, of which 24 were waited for; matrix products, arithmetic and copies ran while one was open for 9% of the time, Pallas kernels for 0%

profile of v1, /device:TPU:0, one launch (start us, length us, event | category | flops | bytes accessed | tf_op | source)
XLA Modules:
  0.0 2750.8 jit_solution(16696924188059355251)
XLA Ops:
  10.8 9.6 all-gather
  20.4 8.4 all-gather.1
  36.9 45.8 %all-gather.9.cloned.1.call-done = bf16[1536,2048]{1,0:T(8,128)(2,1)} async-done(((bf16[384,2048]{1,0:T(8,128)(2,1)}), bf16[1536,2048]{1,0:T(8,128)(2,1)}) %all-gather.9.cloned.1.call-update) | async-done | bytes 6291472 | tf_op jit(solution)/shard_map/all_gather | solution.py:170
  90.2 44.3 %while.44 = (s32[]{:T(128)}, f32[1,2,6,128]{3,2,1,0:T(8,128)S(1)}, f32[1,2,6,128]{3,2,1,0:T(8,128)S(1)}, f32[1,2,6,128,128]{4,3,2,1,0:T(8,128)S(1)}, bf16[2,1,12...) while((s32[]{:T(128)}, f32[1,2,6,128]{3,2,1,0:T(8,128)S(1)}, ...), condition=%wide.region_6.7_spmd.clone, body=%wide.region_2.6_spmd.clone.sunk | while | flops 102664848 | bytes 5382022 | solution.py:211
  145.8 244.7 %all-gather.13.cloned.1.call-done = bf16[1536,8960]{1,0:T(8,128)(2,1)} async-done(((bf16[384,8960]{1,0:T(8,128)(2,1)}), bf16[1536,8960]{1,0:T(8,128)(2,1)}) %all-gather.13.cloned.1.call-update) | async-done | bytes 27525136 | tf_op jit(solution)/shard_map/all_gather | solution.py:229
  390.4 15.8 fusion.105
  406.3 232.9 %all-gather.15.cloned.1.call-done = bf16[1536,8960]{1,0:T(8,128)(2,1)} async-done(((bf16[384,8960]{1,0:T(8,128)(2,1)}), bf16[1536,8960]{1,0:T(8,128)(2,1)}) %all-gather.15.cloned.1.call-update) | async-done | bytes 27525136 | tf_op jit(solution)/shard_map/all_gather | solution.py:230
  639.2 15.8 fusion.106
  655.0 232.9 %all-gather.17.cloned.1.call-done = bf16[8960,1536]{1,0:T(8,128)(2,1)} async-done(((bf16[2240,1536]{1,0:T(8,128)(2,1)}), bf16[8960,1536]{1,0:T(8,128)(2,1)}) %all-gather.17.cloned.1.call-update) | async-done | bytes 27525136 | tf_op jit(solution)/shard_map/all_gather | solution.py:245
  887.9 17.9 multiply_convert_fusion
  905.8 15.6 fusion.107
  921.4 16.4 multiply_reduce_fusion
  945.3 79.4 %while.45 = (s32[]{:T(128)}, f32[1,2,6,128,128]{4,3,2,1,0:T(8,128)S(1)}, bf16[2,1,128,2,128]{4,2,3,1,0:T(8,128)(2,1)S(1)}, f32[2,1,128,2,128]{4,2,3,1,0:T(8,128)...) while((s32[]{:T(128)}, ...), condition=%wide.region_15.16_spmd.clone, body=%wide.region_13.15_spmd.clone.sunk | while | flops 254207632 | bytes 9553853 | solution.py:307
  1043.6 49.2 %fusion.44 = f32[1536,17920]{1,0:T(8,128)} fusion(bf16[128,1536]{1,0:T(8,128)(2,1)S(1)} %copy-done.16, bf16[128,8960]{1,0:T(8,128)(2,1)} %get-tuple-element.822, bf16[128,8960]{1,0:T(8,128)(2,1)S(1)} %copy-done.3), kind=kOutput, calls=%fused_computation.75 | convolution fusion | flops 7055605760 | bytes 115081216 | tf_op jit(solution)/shard_map/rd,rf->df/dot_general | solution.py:262
  1094.5 22.3 fusion.76
  1118.7 173.9 %collective-permute-done.3 = bf16[2240,1536]{1,0:T(8,128)(2,1)S(1)} collective-permute-done((bf16[2240,1536]{1,0:T(8,128)(2,1)}, bf16[2240,1536]{1,0:T(8,128)(2,1)S(1)}, u32[]{:S(2)}, u32[]{:S(2)}) %collective-permute-start.3) | collective-permute-done | bytes 6881312 | tf_op jit(solution)/shard_map/ppermute | solution.py:20
  1292.6 10.3 pad_maximum_fusion.1
  1314.7 345.8 %collective-permute-done.4 = bf16[4480,1536]{1,0:T(8,128)(2,1)} collective-permute-done((bf16[4480,1536]{1,0:T(8,128)(2,1)}, bf16[4480,1536]{1,0:T(8,128)(2,1)}, u32[]{:S(2)}, u32[]{:S(2)}) %collective-permute-start.4) | collective-permute-done | bytes 13762592 | tf_op jit(solution)/shard_map/ppermute | solution.py:20
  1660.4 13.0 constant_dynamic-update-slice_fusion.3
  1680.1 13.7 constant_dynamic-update-slice_fusion
  1696.4 54.4 %all-reduce.4 = (f32[1536]{0:T(1024)S(1)}, f32[2048]{0:T(1024)S(1)}, f32[1536]{0:T(1024)S(1)}) all-reduce(f32[1536]{0:T(1024)S(1)} %get-tuple-element.771, f32[2048]{0:T(1024)S(1)} %convert_reduce_fusion, f32[1536]{0:T(1024)S(1)} %copy-done.35), channel_id=2, replica_groups=mesh['dp'=4,'ctx'=8] {'dp','ctx'}, use_global_device_ids=true, to_apply=%region_18.19.clone | all-reduce | flops 5120 | bytes 40960
  1753.8 19.1 fusion.54
  1776.4 501.0 %reduce-scatter.8.cloned.1.call-done = f32[48,17920]{1,0:T(8,128)} async-done(((f32[1536,17920]{1,0:T(8,128)}), f32[48,17920]{1,0:T(8,128)}) %reduce-scatter.8.cloned.1.call-update) | async-done | bytes 3440656 | tf_op jit(solution)/shard_map/reduce_scatter | solution.py:261
  2281.4 462.2 %reduce-scatter.10.cloned.1.call-done = f32[280,1536]{1,0:T(8,128)} async-done(((f32[8960,1536]{1,0:T(8,128)}), f32[280,1536]{1,0:T(8,128)}) %reduce-scatter.10.cloned.1.call-update) | async-done | bytes 1720336
  (426 shorter events, 212.2 us)
Async XLA Ops:
  7.2 75.5 %all-gather.9.cloned.1.call-start = ((), (), s32[]{:S(2)}) async-start(), calls=%async_computation.3 | async-start | bytes 7864320 | tf_op jit(solution)/shard_map/all_gather | solution.py:170
  7.9 133.6 %all-gather.11.cloned.1.call-start = ((), (), s32[]{:S(2)}) async-start(), calls=%async_computation.4 | async-start | bytes 5898240 | tf_op jit(solution)/shard_map/all_gather | solution.py:172
  8.7 381.8 %all-gather.13.cloned.1.call-start = ((), (), s32[]{:S(2)}) async-start(), calls=%async_computation.5 | async-start | bytes 34406400 | tf_op jit(solution)/shard_map/all_gather | solution.py:229
  9.5 629.7 %all-gather.15.cloned.1.call-start = ((), (), s32[]{:S(2)}) async-start(), calls=%async_computation.6 | async-start | bytes 34406400 | tf_op jit(solution)/shard_map/all_gather | solution.py:230
  10.0 877.9 %all-gather.17.cloned.1.call-start = ((), (), s32[]{:S(2)}) async-start(), calls=%async_computation.7 | async-start | bytes 34406400 | tf_op jit(solution)/shard_map/all_gather | solution.py:245
  10.6 1762.3 %reduce-scatter.6.cloned.1.call-start = ((), (), s32[]{:S(2)}) async-start(), calls=%async_computation.8 | async-start | bytes 22708224 | tf_op jit(solution)/shard_map/reduce_scatter | solution.py:324
  97.0 6.2 collective-permute-start
  103.2 6.2 collective-permute-start
  109.5 6.2 collective-permute-start
  115.7 6.2 collective-permute-start
  122.0 6.2 collective-permute-start
  128.2 6.2 collective-permute-start
  945.3 9.9 collective-permute-start.1
  955.2 9.9 collective-permute-start.1
  965.1 9.9 collective-permute-start.1
  975.0 9.9 collective-permute-start.1
  984.9 9.9 collective-permute-start.1
  994.8 9.9 collective-permute-start.1
  1004.7 9.9 collective-permute-start.1
  1014.7 9.9 collective-permute-start.1
  1041.9 1235.5 %reduce-scatter.8.cloned.1.call-start = ((), (), s32[]{:S(2)}) async-start(), calls=%async_computation.9 | async-start | bytes 113541120 | tf_op jit(solution)/shard_map/reduce_scatter | solution.py:261
  1092.9 1650.7 %reduce-scatter.10.cloned.1.call-start = ((), (), s32[]{:S(2)}) async-start(), calls=%async_computation.10 | async-start | bytes 56770560
  1116.8 175.8 %collective-permute-start.3 = (bf16[2240,1536]{1,0:T(8,128)(2,1)}, bf16[2240,1536]{1,0:T(8,128)(2,1)S(1)}, u32[]{:S(2)}, u32[]{:S(2)}) collective-permute-start(bf16[2240,1536]{1,0:T(8,128)(2,1)} %param.27), channel_id=1, source_target_pairs={{0,24},{8,0},{16,8},{24,16},{1,25},{9,1},{17,9},{25,17},{2,26},{10... | collective-permute-start | bytes 20643848 | tf_op jit(solution)/shard_map/ppermute | solution.py:20
  1302.9 357.5 %collective-permute-start.4 = (bf16[4480,1536]{1,0:T(8,128)(2,1)}, bf16[4480,1536]{1,0:T(8,128)(2,1)}, u32[]{:S(2)}, u32[]{:S(2)}) collective-permute-start(bf16[4480,1536]{1,0:T(8,128)(2,1)} %pad_maximum_fusion.1), channel_id=1, source_target_pairs={{0,16},{8,24},{16,0},{24,8},{1,17},{9,25},{17,1},{25,9},{2,18},{10... | collective-permute-start | bytes 41287688 | tf_op jit(solution)/shard_map/ppermute | solution.py:20
  (61 other events, 3614.4 us)
Sparse Core Ops, SparseCore 0:
  9.8 72.8 all-gather.8
  84.5 56.9 all-gather.10
  143.4 247.0 all-gather.12
  392.1 246.9 all-gather.14
  640.9 246.9 all-gather.16
  1042.1 354.5 reduce-scatter.5
  1403.0 874.3 reduce-scatter.7
  2284.4 459.0 reduce-scatter.9
